TPU v7x, 32 devices: a whole 2x2x4 slice. The times are simulated.
32 devices in a mesh: groups: 2 (over y), vox: 4 (over z), freq: 2 (over x), sub: 2 (over core).
Axes of the slice: x: 2, y: 2, z: 4, core: 2. Of those that a mesh axis runs over, the one named last changes fastest.
Arguments:
- residual: bfloat16 [4, 1024, 1024], P(('groups', 'freq'), 'vox', 'sub'), parts along dimension 0, may hold values from -6 to 6
- green: bfloat16 [4, 1024, 8192], P(('groups', 'freq'), None, 'vox'), parts along dimension 0, may hold values from -0.15625 to 0.15625
- active: int32 [4, 1024], P(('groups', 'freq')), parts along dimension 0, may hold values 0 or 1
- aperture: int32 [4], P(('groups', 'freq')), parts along dimension 0, may hold values from 256 to 511
- step_gain: float32 [4], P(('groups', 'freq')), parts along dimension 0, may hold values from 6 to 24
- block_region: int32 [128], P(('groups', 'vox')), parts along dimension 0, may hold values from 0 to 15
- strength: float32 [16], replicated, may hold values from 0.1 to 1
Outputs:
- updated: float32 [4, 1024, 1024], P(('groups', 'freq'), 'vox', 'sub'), parts along dimension 0
There are 2 independent parts, one for each index of `groups`. A program takes and returns all parts, laid end to end along the dimension named above; an argument that names none is the same for every part. Nothing has to cross between parts.
All inputs are finite; a program needn't handle non-finite values. No bound on the sum of `active` on one device may be relied on, other than what follows from the above.
Results may differ from a plain program's by a relative error of at most 0.0026.
Values may be sent and summed in bfloat16 or wider, within the bound.
A program may use at most 64 MiB of HBM per device.

v0:
```python
import jax
import jax.numpy as jnp
from jax import lax
from jax.sharding import PartitionSpec as P

BLOCK = 128
REGIONS = 16


smooth_sq = 0.0625


def penalize(image_sum, strength_map):
    return image_sum - strength_map * image_sum / jnp.sqrt(image_sum * image_sum + smooth_sq)


def body(residual, green, active, aperture, step_gain, block_region, strength):
    local_data = residual[0]
    green_rows = green[0]
    element_on = active[0]
    rows_local = local_data.shape[0]
    cols_local = local_data.shape[1]
    row_start = lax.axis_index("vox") * rows_local
    col_start = lax.axis_index("sub") * cols_local
    row_ids = row_start + jnp.arange(rows_local, dtype=jnp.int32)
    col_ids = col_start + jnp.arange(cols_local, dtype=jnp.int32)
    row_on = lax.dynamic_slice_in_dim(element_on, row_start, rows_local)
    col_on = lax.dynamic_slice_in_dim(element_on, col_start, cols_local)
    in_band = (jnp.abs(row_ids[:, None] - col_ids[None, :]) <= aperture[0]).astype(jnp.int32)
    pair_mask = row_on[:, None] * col_on[None, :] * in_band
    masked = local_data * pair_mask.astype(jnp.bfloat16)
    tx_green = lax.dynamic_slice_in_dim(green_rows, col_start, cols_local, 0)
    rx_green = green_rows
    beamed = lax.dot_general(
        lax.all_gather(masked, "vox", axis=0, tiled=True),
        rx_green,
        (((0,), (0,)), ((), ())),
        preferred_element_type=jnp.float32,
    )
    partial_value = jnp.sum(tx_green.astype(jnp.float32) * beamed, axis=0)
    region_ids = jnp.arange(REGIONS, dtype=jnp.int32)
    onehot = (block_region[:, None] == region_ids[None, :]).astype(jnp.float32)
    block_strength = jnp.dot(onehot, strength, precision=lax.Precision.HIGHEST)
    strength_map = jnp.broadcast_to(
        block_strength[:, None], (block_region.shape[0], BLOCK)
    ).reshape(-1)
    image_sum = lax.psum(partial_value, ("freq", "sub"))
    scaled = penalize(image_sum, strength_map)
    weighted = (tx_green.astype(jnp.float32) * scaled[None, :]).astype(jnp.bfloat16)
    rx_green = green_rows
    gradient = lax.psum_scatter(
        lax.dot_general(
            rx_green, weighted, (((1,), (1,)), ((), ())), preferred_element_type=jnp.float32
        ),
        "vox",
        scatter_dimension=0,
        tiled=True,
    )
    updated = pair_mask.astype(jnp.float32) * (
        local_data.astype(jnp.float32) - step_gain[0] * gradient
    )
    return updated[None]


def solution(mesh):
    in_specs = (
        P(("groups", "freq"), "vox", "sub"),
        P(("groups", "freq"), None, "vox"),
        P(("groups", "freq"), None),
        P(("groups", "freq")),
        P(("groups", "freq")),
        P(("groups", "vox")),
        P(),
    )
    out_specs = P(("groups", "freq"), "vox", "sub")
    return jax.shard_map(body, mesh=mesh, in_specs=in_specs, out_specs=out_specs, check_vma=False)
```

profile of v0, /device:TPU:0, one launch (start us, length us, event | category | flops | bytes accessed | tf_op | source)
XLA Modules:
  0.0 112.0 jit_solution(282476886270664636)
XLA Ops:
  6.5 0.0 copy-start
  6.5 0.0 all-gather.2.cloned.1.call-start
  6.5 0.7 copy-done
  7.2 1.1 copy.8
  9.0 1.0 fusion.19
  9.9 0.0 all-gather.2.cloned.1.call-update
  9.9 0.0 reduce-scatter.2.cloned.1.call-start
  10.0 0.9 convolution_bitcast_fusion
  10.9 31.9 %all-gather.2.cloned.1.call-done = bf16[1024,512]{0,1:T(8,128)(2,1)} async-done(((bf16[256,512]{0,1:T(8,128)(2,1)}), bf16[1024,512]{0,1:T(8,128)(2,1)}) %all-gather.2.cloned.1.call-update) | async-done | bytes 1048592 | tf_op jit(solution)/shard_map/all_gather | solution.py:35
  42.8 5.5 %fusion.2 = f32[2048]{0:T(1024)S(1)} fusion(bf16[1,1024,2048]{2,1,0:T(8,128)(2,1)} %param.8, s32[]{:T(128)S(6)} %select_n.8, bf16[1024,512]{0,1:T(8,128)(2,1)} %all-gather.2.cloned.1.call-done), kind=kOutput, calls=%fused_computation.4 | convolution fusion | flops 2150627328 | bytes 7348228 | tf_op jit(solution)/shard_map/dot_general | solution.py:34
  48.3 6.2 %psum.7 = f32[2048]{0:T(1024)S(1)} all-reduce(f32[2048]{0:T(1024)S(1)} %fusion.2), channel_id=1, replica_groups=mesh['groups'=2,'vox'=4,'freq'=2,'sub'=2] {'freq','sub'}, use_global_device_ids=true, to_apply=%region_1.0 | all-reduce | flops 2048 | bytes 16384 | tf_op jit(solution)/shard_map/psum | solution.py:47
  54.5 0.1 fusion.21
  54.6 6.5 %fusion.11 = f32[1024,512]{0,1:T(8,128)} fusion(bf16[1,1024,2048]{2,1,0:T(8,128)(2,1)} %param.8, f32[2048]{0:T(1024)S(1)} %fusion.21, s32[]{:T(128)S(6)} %select_n.8), kind=kOutput, calls=%fused_computation.12 | convolution fusion | flops 2150629376 | bytes 8396804 | tf_op jit(solution)/shard_map/dot_general | solution.py:52
  61.1 0.0 reduce-scatter.2.cloned.1.call-update
  61.8 41.1 %reduce-scatter.2.cloned.1.call-done = f32[256,512]{0,1:T(8,128)} async-done(((f32[1024,512]{0,1:T(8,128)}), f32[256,512]{0,1:T(8,128)}) %reduce-scatter.2.cloned.1.call-update) | async-done | bytes 524304 | tf_op jit(solution)/shard_map/reduce_scatter | solution.py:51
  102.9 1.3 %multiply_bitcast_fusion = f32[1,256,512]{1,2,0:T(8,128)S(1)} fusion(f32[256,512]{0,1:T(8,128)} %reduce-scatter.2.cloned.1.call-done, bf16[1,256,512]{1,2,0:T(8,128)(2,1)S(1)} %copy.8, f32[]{:T(128)} %bitcast.45, s32[512]{0:T(512)S(1)} %bitcast.47, s32[256]{0:T(256)S(1)} %bitcast.49, s32[]{:T(128)} %bitcast.43, s32[512]{0:T(512)S(1)} %iota_add_fusion, ...), kind=kLoop, calls=%fused_computation.14 | loop fusion | flops 1310720 | bytes 1316872 | tf_op jit(solution)/shard_map/broadcast_in_dim | solution.py:62
  104.2 1.0 copy.9
  (4 shorter events, 0.0 us)
Async XLA Ops:
  6.5 0.7 copy-start
  6.5 36.2 %all-gather.2.cloned.1.call-start = ((), (), s32[]{:S(2)}) async-start(), calls=%async_computation.1 | async-start | bytes 1310720 | tf_op jit(solution)/shard_map/all_gather | solution.py:35
  9.9 92.9 %reduce-scatter.2.cloned.1.call-start = ((), (), s32[]{:S(2)}) async-start(), calls=%async_computation.2 | async-start | bytes 2621440 | tf_op jit(solution)/shard_map/reduce_scatter | solution.py:51
Sparse Core Ops, SparseCore 0:
  10.1 32.6 all-gather.1
  61.3 41.5 reduce-scatter.1
where the time goes:
time: 112 us
  waiting for transfers between devices  73 us (65%)
  between operations  14.7 us (13%)
  matrix products  12.9 us (12%)
  blocking collectives  6.23 us (6%)
  local copies, waits for them, and re-layouts  2.75 us (2%)
  other arithmetic  2.33 us (2%)
    reduce_scatter x1, waiting for transfers between devices, body(): lax.psum_scatter(lax.dot_general(rx_green, weighted, (((1,), (1,)), ((),...  41.1 us
    all_gather x1, waiting for transfers between devices, body(): lax.all_gather(masked, 'vox', axis=0, tiled=True)  31.9 us
    dot_general x1, matrix products, body(): lax.dot_general(rx_green, weighted, (((1,), (1,)), ((), ())), preferred_e...  6.55 us
    psum x1, blocking collectives, body(): image_sum = lax.psum(partial_value, ('freq', 'sub'))  6.23 us
    dot_general x1, matrix products, body(): lax.dot_general(lax.all_gather(masked, 'vox', axis=0, tiled=True), rx_gre...  5.52 us
  transfers between devices with their start and end apart: 2, of which 2 were waited for; matrix products, arithmetic and copies ran while one was open for 1% of the time, Pallas kernels for 0%

commit v1 on v0

v1 whole, which is shorter than its diff:
```python
import jax
import jax.numpy as jnp
from jax import lax
from jax.experimental import pallas as pl
from jax.experimental.pallas import tpu as pltpu
from jax.sharding import PartitionSpec as P

BLOCK = 128
LANES = 128
APERTURE_MAX = 511
smooth_sq = 0.0625
MESH = pl.DeviceIdType.MESH


def penalize(image_sum, strength_map):
    return image_sum - strength_map * image_sum / jnp.sqrt(image_sum * image_sum + smooth_sq)


def make_kernel(n, nf, ns, rows, cols, ne, vox_local, n_blocks):
    tile = min(rows, LANES)
    per = rows // tile
    col_tiles = cols // LANES
    vchunk = min(512, vox_local)
    peers = nf * ns

    def kernel(
        res, green, active, aperture, gain, region, strength, out,
        allm, gv, act_col, mm, img, ar_send, ar_land, wgt, gacc, send_buf, land_r, land_l,
        sem_g, sem_own, agr_s, agr_r, agl_s, agl_r, ar_s, ar_r, rsr_s, rsr_r, rsl_s, rsl_r,
    ):
        z = lax.axis_index("vox")
        f = lax.axis_index("freq")
        s = lax.axis_index("sub")
        has_up = z < n - 1
        has_down = z > 0
        up = {"vox": jnp.minimum(z + 1, n - 1)}
        down = {"vox": jnp.maximum(z - 1, 0)}

        def row_of(block):
            return pl.multiple_of(block * rows, rows)

        own_copy = pltpu.make_async_copy(res, allm.at[pl.ds(row_of(z), rows), :], sem_own)
        own_copy.start()
        green_copy = pltpu.make_async_copy(green, gv, sem_g)
        green_copy.start()

        def peer(k):
            df, ds = k // ns, k % ns
            return {"freq": lax.rem(f + df, nf), "sub": lax.rem(s + ds, ns)}

        barrier = pltpu.get_barrier_semaphore()
        for k in range(1, peers):
            pl.semaphore_signal(barrier, inc=1, device_id=peer(k), device_id_type=MESH)

        @pl.when(has_up)
        def _():
            pl.semaphore_signal(barrier, inc=1, device_id=up, device_id_type=MESH)

        @pl.when(has_down)
        def _():
            pl.semaphore_signal(barrier, inc=1, device_id=down, device_id_type=MESH)

        pl.semaphore_wait(barrier, peers - 1 + has_up.astype(jnp.int32) + has_down.astype(jnp.int32))

        def band(q):
            r0 = q * tile
            first = jnp.int32(0)
            count = jnp.int32(0)
            for j in range(col_tiles):
                c0 = s * cols + j * LANES
                below = c0 + LANES - 1 + APERTURE_MAX < r0
                above = c0 > r0 + tile - 1 + APERTURE_MAX
                first = first + below.astype(jnp.int32)
                count = count + 1 - below.astype(jnp.int32) - above.astype(jnp.int32)
            return first, count

        def per_width(q, fn):
            first, count = band(q)
            for w in range(1, col_tiles + 1):
                @pl.when(count == w)
                def _(w=w):
                    fn(pl.ds(pl.multiple_of(first * LANES, LANES), w * LANES))

        def tile_rows(q):
            return pl.ds(pl.multiple_of(q * tile, tile), tile)

        def remote(src, dst, send, recv, target):
            return pltpu.make_async_remote_copy(
                src_ref=src, dst_ref=dst, send_sem=send, recv_sem=recv,
                device_id=target, device_id_type=MESH,
            )

        def gather_up(q, c):
            a = allm.at[tile_rows(q), c]
            return remote(a, a, agr_s.at[q], agr_r.at[q], up)

        def gather_down(q, c):
            a = allm.at[tile_rows(q), c]
            return remote(a, a, agl_s.at[q], agl_r.at[q], down)

        for t in range(per):
            q = z * per + t

            def first_up(c, q=q, t=t):
                remote(res.at[pl.ds(t * tile, tile), c], allm.at[tile_rows(q), c],
                       agr_s.at[q], agr_r.at[q], up).start()

            def first_down(c, q=q, t=t):
                remote(res.at[pl.ds(t * tile, tile), c], allm.at[tile_rows(q), c],
                       agl_s.at[q], agl_r.at[q], down).start()

            @pl.when(has_up)
            def _():
                per_width(q, first_up)

            @pl.when(has_down)
            def _():
                per_width(q, first_down)

        for i in range(ne // LANES):
            line = active[0:1, i * LANES:(i + 1) * LANES].astype(jnp.float32)
            act_col[i * LANES:(i + 1) * LANES, :] = jnp.broadcast_to(line, (LANES, LANES)).T
        img[...] = jnp.zeros_like(img)
        col0 = pl.multiple_of(s * cols, cols)

        def pair_mask(block):
            r0 = row_of(block)
            rr = lax.broadcasted_iota(jnp.int32, (rows, cols), 0) + r0
            cc = lax.broadcasted_iota(jnp.int32, (rows, cols), 1) + col0
            in_band = jnp.abs(rr - cc) <= aperture[0]
            row_on = act_col[pl.ds(r0, rows), 0:1] > 0.5
            col_on = active[0:1, pl.ds(col0, cols)] > 0
            return in_band & row_on & col_on

        def image_part(block):
            r0 = row_of(block)
            value = allm[pl.ds(r0, rows), :].astype(jnp.float32)
            mm[...] = jnp.where(pair_mask(block), value, 0.0).astype(jnp.bfloat16)

            @pl.loop(0, vox_local // vchunk)
            def _(v):
                vs = pl.ds(pl.multiple_of(v * vchunk, vchunk), vchunk)
                y = jnp.dot(mm[...], gv[pl.ds(col0, cols), vs], preferred_element_type=jnp.float32)
                y = y * gv[pl.ds(r0, rows), vs].astype(jnp.float32)
                img[:, vs] += jnp.sum(y.reshape(rows // 8, 8, vchunk), axis=0)

        own_copy.wait()
        green_copy.wait()
        image_part(z)

        @pl.loop(0, n - 1)
        def _(step):
            from_below = z - 1 - step
            from_above = z + 1 + step
            for t in range(per):
                @pl.when(from_below >= 0)
                def _():
                    q = from_below * per + t

                    def land(c):
                        gather_up(q, c).wait_recv()

                        @pl.when(has_up)
                        def _():
                            gather_up(q, c).start()
                    per_width(q, land)

                @pl.when(from_above < n)
                def _():
                    q = from_above * per + t

                    def land(c):
                        gather_down(q, c).wait_recv()

                        @pl.when(has_down)
                        def _():
                            gather_down(q, c).start()
                    per_width(q, land)

            @pl.when(from_below >= 0)
            def _():
                image_part(from_below)

            @pl.when(from_above < n)
            def _():
                image_part(from_above)

        ar_send[...] = jnp.sum(img[...], axis=0, keepdims=True)
        exchanges = [
            remote(ar_send, ar_land.at[k], ar_s.at[k], ar_r.at[k], peer(k)) for k in range(1, peers)
        ]
        for e in exchanges:
            e.start()
        strength_map = jnp.concatenate(
            [jnp.full((1, BLOCK), strength[region[b]], jnp.float32) for b in range(n_blocks)], axis=1
        )
        for e in exchanges:
            e.wait_recv()
        total = ar_send[...]
        for k in range(1, peers):
            total = total + ar_land[k]
        img[0:1, :] = penalize(total, strength_map)

        wrows = 32

        @pl.loop(0, cols // wrows)
        def _(i):
            src = pl.ds(pl.multiple_of(col0 + i * wrows, wrows), wrows)
            dst = pl.ds(pl.multiple_of(i * wrows, wrows), wrows)
            wgt[dst, :] = (gv[src, :].astype(jnp.float32) * img[0:1, :]).astype(jnp.bfloat16)

        def scatter_up(q, c):
            return remote(send_buf.at[tile_rows(q), c], land_r.at[tile_rows(q), c],
                          rsr_s.at[q], rsr_r.at[q], up)

        def scatter_down(q, c):
            return remote(send_buf.at[tile_rows(q), c], land_l.at[tile_rows(q), c],
                          rsl_s.at[q], rsl_r.at[q], down)

        def each_tile(block, make, act):
            for t in range(per):
                q = block * per + t
                per_width(q, lambda c, q=q: act(make(q, c)))

        def partial_step(k, ends):
            lo, hi = ends
            use_hi = (hi > z) & ((lo >= z) | (z + (n - 1 - hi) <= (n - 1 - z) + lo))
            d = jnp.where(use_hi, hi, lo)
            rs = pl.ds(row_of(d), rows)
            part = lax.dot_general(
                gv[rs, :], wgt[...], (((1,), (1,)), ((), ())), preferred_element_type=jnp.float32
            )
            gacc[rs, :] = part
            sends_up = (d > z) & jnp.logical_not(has_down)
            sends_down = (d < z) & jnp.logical_not(has_up)

            @pl.when(sends_up | sends_down)
            def _():
                send_buf[rs, :] = part.astype(jnp.bfloat16)

            @pl.when(sends_up)
            def _():
                each_tile(d, scatter_up, lambda c: c.start())

            @pl.when(sends_down)
            def _():
                each_tile(d, scatter_down, lambda c: c.start())

            step_hi = use_hi.astype(jnp.int32)
            return lo + 1 - step_hi, hi - step_hi

        lax.fori_loop(0, n, partial_step, (jnp.int32(0), jnp.int32(n - 1)))

        @pl.loop(0, n - 1)
        def _(slot):
            @pl.when(has_down & (slot >= z))
            def _():
                d = z + n - 1 - slot
                for t in range(per):
                    q = d * per + t

                    def add(c):
                        scatter_up(q, c).wait_recv()
                        send_buf[tile_rows(q), c] = (
                            gacc[tile_rows(q), c] + land_r[tile_rows(q), c].astype(jnp.float32)
                        ).astype(jnp.bfloat16)
                        scatter_up(q, c).start()
                    per_width(q, add)

            @pl.when(has_up & (slot >= n - 1 - z))
            def _():
                d = slot - (n - 1 - z)
                for t in range(per):
                    q = d * per + t

                    def add(c):
                        scatter_down(q, c).wait_recv()
                        send_buf[tile_rows(q), c] = (
                            gacc[tile_rows(q), c] + land_l[tile_rows(q), c].astype(jnp.float32)
                        ).astype(jnp.bfloat16)
                        scatter_down(q, c).start()
                    per_width(q, add)

        @pl.when(has_down)
        def _():
            each_tile(z, scatter_up, lambda c: c.wait_recv())

        @pl.when(has_up)
        def _():
            each_tile(z, scatter_down, lambda c: c.wait_recv())

        mine = pl.ds(row_of(z), rows)
        gradient = gacc[mine, :]
        gradient = gradient + jnp.where(has_down, land_r[mine, :].astype(jnp.float32), 0.0)
        gradient = gradient + jnp.where(has_up, land_l[mine, :].astype(jnp.float32), 0.0)
        data = allm[mine, :].astype(jnp.float32)
        out[...] = jnp.where(pair_mask(z), data - gain[0] * gradient, 0.0)

        for e in exchanges:
            e.wait_send()

        @pl.loop(0, n)
        def _(b):
            @pl.when(has_up & (b <= z))
            def _():
                each_tile(b, gather_up, lambda c: c.wait_send())

            @pl.when(has_down & (b >= z))
            def _():
                each_tile(b, gather_down, lambda c: c.wait_send())

            @pl.when(has_up & (b > z))
            def _():
                each_tile(b, scatter_up, lambda c: c.wait_send())

            @pl.when(has_down & (b < z))
            def _():
                each_tile(b, scatter_down, lambda c: c.wait_send())

    tiles = n * per
    dma = pltpu.SemaphoreType.DMA
    scratch = [
        pltpu.VMEM((ne, cols), jnp.bfloat16),
        pltpu.VMEM((ne, vox_local), jnp.bfloat16),
        pltpu.VMEM((ne, LANES), jnp.float32),
        pltpu.VMEM((rows, cols), jnp.bfloat16),
        pltpu.VMEM((8, vox_local), jnp.float32),
        pltpu.VMEM((1, vox_local), jnp.float32),
        pltpu.VMEM((peers, 1, vox_local), jnp.float32),
        pltpu.VMEM((cols, vox_local), jnp.bfloat16),
        pltpu.VMEM((ne, cols), jnp.float32),
        pltpu.VMEM((ne, cols), jnp.bfloat16),
        pltpu.VMEM((ne, cols), jnp.bfloat16),
        pltpu.VMEM((ne, cols), jnp.bfloat16),
        dma, dma,
        dma((tiles,)), dma((tiles,)), dma((tiles,)), dma((tiles,)),
        dma((peers,)), dma((peers,)),
        dma((tiles,)), dma((tiles,)), dma((tiles,)), dma((tiles,)),
    ]
    return kernel, scratch


def solution(mesh):
    sizes = dict(mesh.shape)

    def body(residual, green, active, aperture, step_gain, block_region, strength):
        _, rows, cols = residual.shape
        _, ne, vox_local = green.shape
        kernel, scratch = make_kernel(
            sizes["vox"], sizes["freq"], sizes["sub"], rows, cols, ne, vox_local,
            block_region.shape[0],
        )
        vmem = pl.BlockSpec(memory_space=pltpu.VMEM)
        smem = pl.BlockSpec(memory_space=pltpu.SMEM)
        any_space = pl.BlockSpec(memory_space=pl.ANY)
        updated = pl.pallas_call(
            kernel,
            out_shape=jax.ShapeDtypeStruct((rows, cols), jnp.float32),
            in_specs=[any_space, any_space, vmem, smem, smem, smem, smem],
            out_specs=vmem,
            scratch_shapes=scratch,
            compiler_params=pltpu.CompilerParams(
                collective_id=0, has_side_effects=True, vmem_limit_bytes=48 * 1024 * 1024
            ),
            name="imaging_step",
        )(residual[0], green[0], active, aperture, step_gain, block_region, strength)
        return updated[None]

    in_specs = (
        P(("groups", "freq"), "vox", "sub"),
        P(("groups", "freq"), None, "vox"),
        P(("groups", "freq"), None),
        P(("groups", "freq")),
        P(("groups", "freq")),
        P(("groups", "vox")),
        P(),
    )
    out_specs = P(("groups", "freq"), "vox", "sub")
    return jax.shard_map(body, mesh=mesh, in_specs=in_specs, out_specs=out_specs, check_vma=False)
```

time: 112 us -> 51.8 us (0.46)
  waiting for transfers between devices: 73 us -> 0 us
  Pallas kernels: 0 us -> 44.3 us
  between operations: 14.7 us -> 1.32 us
  matrix products: 12.9 us -> 0 us
  blocking collectives: 6.23 us -> 0 us
  local copies, waits for them, and re-layouts: 2.75 us -> 5.92 us
  other arithmetic: 2.33 us -> 0 us
    pallas_call x0 -> x1, Pallas kernels: none -> 44.3 us  [body(): pl.pallas_call(kernel, out_shape=jax.ShapeDtypeStruct((rows, cols), jnp.f...]
    reduce_scatter x1 -> x0, waiting for transfers between devices: 41.1 us -> none  [body(): lax.psum_scatter(lax.dot_general(rx_green, weighted, (((1,), (1,)), ((),...]
    all_gather x1 -> x0, waiting for transfers between devices: 31.9 us -> none  [body(): lax.all_gather(masked, 'vox', axis=0, tiled=True)]
    dot_general x3 -> x0, matrix products: 12.9 us -> none  [the longest x1 6.55 us: body(): lax.dot_general(rx_green, weighted, (((1,), (1,)), ((), ())), preferred_e...]
    psum x1 -> x0, blocking collectives: 6.23 us -> none  [body(): image_sum = lax.psum(partial_value, ('freq', 'sub'))]
    unnamed x3 -> x11, local copies, waits for them, and re-layouts: 1.76 us -> 5.92 us
    broadcast_in_dim x1 -> x0, other arithmetic: 1.3 us -> none  [body(): return updated[None]]
  transfers between devices with their start and end apart: 2 -> 0, of which waited for: 2 -> 0; matrix products, arithmetic and copies ran while one was open for 1% -> 0% of each run, Pallas kernels for 0% -> 0%
where the time goes in v1:
time: 51.8 us; the launch traced here: 51.5 us
  Pallas kernels  44.3 us (86%)
  local copies, waits for them, and re-layouts  5.92 us (11%)
  between operations  1.32 us (3%)
    pallas_call x1, Pallas kernels, body(): pl.pallas_call(kernel, out_shape=jax.ShapeDtypeStruct((rows, cols), jnp.f...  44.3 us
    unnamed x11, local copies, waits for them, and re-layouts  5.92 us

profile of v1, /device:TPU:0, one launch (start us, length us, event | category | flops | bytes accessed | tf_op | source)
XLA Modules:
  0.0 51.5 jit_solution(16926040441456447705)
XLA Ops:
  1.3 0.0 copy-start
  1.3 2.2 %copy-done = bf16[1,1024,2048]{2,1,0:T(8,128)(2,1)S(1)} copy-done((bf16[1,1024,2048]{2,1,0:T(8,128)(2,1)S(1)}, bf16[1,1024,2048]{2,1,0:T(8,128)(2,1)}, u32[]{:S(2)}) %copy-start) | copy-done | bytes 4194328
  3.5 0.0 copy-start.1
  3.5 0.9 %copy-done.1 = bf16[1,256,512]{2,1,0:T(8,128)(2,1)S(1)} copy-done((bf16[1,256,512]{2,1,0:T(8,128)(2,1)S(1)}, bf16[1,256,512]{2,1,0:T(8,128)(2,1)}, u32[]{:S(2)}) %copy-start.1) | copy-done | bytes 262168
  4.4 0.0 copy-start.2
  4.4 0.7 %copy-done.2 = s32[1,1024]{1,0:T(1,128)S(1)} copy-done((s32[1,1024]{1,0:T(1,128)S(1)}, s32[1,1024]{1,0:T(1,128)}, u32[]{:S(2)}) %copy-start.2) | copy-done | bytes 4120
  5.1 0.0 copy-start.3
  5.1 0.7 %copy-done.3 = s32[16]{0:T(128)S(1)} copy-done((s32[16]{0:T(128)S(1)}, s32[16]{0:T(128)}, u32[]{:S(2)}) %copy-start.3) | copy-done | bytes 88
  5.8 0.0 copy-start.4
  5.8 0.7 %copy-done.4 = f32[16]{0:T(128)S(1)} copy-done((f32[16]{0:T(128)S(1)}, f32[16]{0:T(128)}, u32[]{:S(2)}) %copy-start.4) | copy-done | bytes 88
  6.4 44.3 %imaging_step.1 = f32[256,512]{1,0:T(8,128)S(1)} custom-call(bf16[256,512]{1,0:T(8,128)(2,1)S(1)} %bitcast.5, bf16[1024,2048]{1,0:T(8,128)(2,1)S(1)} %bitcast.3, s32[1,1024]{1,0:T(1,128)S(1)} %copy-done.2, s32[1]{0:T(128)S(6)} %copy.9.aperture, f32[1]{0:T(128)S(6)} %copy.10.gain, s32[16]{0:T(128)S(1)} %copy-done.3, f32[16]{0:T(128)S(1)} %copy-done.4), custom_call_target="tpu_custom_call" | custom-call | tf_op jit(solution)/shard_map/imaging_step/pallas_call | solution.py:356
  50.7 0.8 %copy.11 = f32[1,256,512]{2,1,0:T(8,128)} copy(f32[1,256,512]{2,1,0:T(8,128)S(1)} %bitcast.4) | data formatting | bytes 1048576
Async XLA Ops:
  1.3 2.2 %copy-start = (bf16[1,1024,2048]{2,1,0:T(8,128)(2,1)S(1)}, bf16[1,1024,2048]{2,1,0:T(8,128)(2,1)}, u32[]{:S(2)}) copy-start(bf16[1,1024,2048]{2,1,0:T(8,128)(2,1)} %param.8) | copy-start | bytes 12582916
  3.5 0.9 %copy-start.1 = (bf16[1,256,512]{2,1,0:T(8,128)(2,1)S(1)}, bf16[1,256,512]{2,1,0:T(8,128)(2,1)}, u32[]{:S(2)}) copy-start(bf16[1,256,512]{2,1,0:T(8,128)(2,1)} %param.7) | copy-start | bytes 786436
  4.4 0.7 %copy-start.2 = (s32[1,1024]{1,0:T(1,128)S(1)}, s32[1,1024]{1,0:T(1,128)}, u32[]{:S(2)}) copy-start(s32[1,1024]{1,0:T(1,128)} %active.1) | copy-start | bytes 12292
  5.1 0.7 %copy-start.3 = (s32[16]{0:T(128)S(1)}, s32[16]{0:T(128)}, u32[]{:S(2)}) copy-start(s32[16]{0:T(128)} %region.1) | copy-start | bytes 196
  5.8 0.7 %copy-start.4 = (f32[16]{0:T(128)S(1)}, f32[16]{0:T(128)}, u32[]{:S(2)}) copy-start(f32[16]{0:T(128)} %strength.1) | copy-start | bytes 196

commit v2 on v1

--- a/solution.py
+++ b/solution.py
@@ -9,6 +9,7 @@
 LANES = 128
 APERTURE_MAX = 511
 smooth_sq = 0.0625
+FULL, UP, DOWN = range(3)
 MESH = pl.DeviceIdType.MESH
 
 
@@ -16,7 +17,7 @@
     return image_sum - strength_map * image_sum / jnp.sqrt(image_sum * image_sum + smooth_sq)
 
 
-def make_kernel(n, nf, ns, rows, cols, ne, vox_local, n_blocks):
+def make_kernel(n, nf, ns, rows, cols, ne, vox_local, n_blocks, regions):
     tile = min(rows, LANES)
     per = rows // tile
     col_tiles = cols // LANES
@@ -24,8 +25,9 @@
     peers = nf * ns
 
     def kernel(
-        res, green, active, aperture, gain, region, strength, out,
-        allm, gv, act_col, mm, img, ar_send, ar_land, wgt, gacc, send_buf, land_r, land_l,
+        res, green, active_in, aperture_in, gain_in, region_in, strength_in, out,
+        active, aperture, gain, region, strength, sem_small,
+        allm, gv, act_col, mm, img, ar_send, ar_land, wgt, gacc, flipped, send_buf, land_r, land_l,
         sem_g, sem_own, agr_s, agr_r, agl_s, agl_r, ar_s, ar_r, rsr_s, rsr_r, rsl_s, rsl_r,
     ):
         z = lax.axis_index("vox")
@@ -39,6 +41,15 @@
         def row_of(block):
             return pl.multiple_of(block * rows, rows)
 
+        small = [
+            pltpu.make_async_copy(a, b, sem_small.at[i])
+            for i, (a, b) in enumerate((
+                (active_in, active), (aperture_in, aperture), (gain_in, gain),
+                (region_in, region), (strength_in, strength),
+            ))
+        ]
+        for c in small:
+            c.start()
         own_copy = pltpu.make_async_copy(res, allm.at[pl.ds(row_of(z), rows), :], sem_own)
         own_copy.start()
         green_copy = pltpu.make_async_copy(green, gv, sem_g)
@@ -62,20 +73,30 @@
 
         pl.semaphore_wait(barrier, peers - 1 + has_up.astype(jnp.int32) + has_down.astype(jnp.int32))
 
-        def band(q):
+        def square(q):
+            local = q * tile - s * cols
+            inside = (local >= 0) & (local < cols)
+            return inside, jnp.clip(local, 0, cols - 1) // LANES
+
+        def band(q, kind):
             r0 = q * tile
+            inside, diag = square(q)
             first = jnp.int32(0)
             count = jnp.int32(0)
             for j in range(col_tiles):
                 c0 = s * cols + j * LANES
                 below = c0 + LANES - 1 + APERTURE_MAX < r0
                 above = c0 > r0 + tile - 1 + APERTURE_MAX
+                if kind == UP:
+                    above = above | (inside & (j > diag))
+                if kind == DOWN:
+                    below = below | (inside & (j < diag))
                 first = first + below.astype(jnp.int32)
                 count = count + 1 - below.astype(jnp.int32) - above.astype(jnp.int32)
             return first, count
 
-        def per_width(q, fn):
-            first, count = band(q)
+        def per_width(q, fn, kind=FULL):
+            first, count = band(q, kind)
             for w in range(1, col_tiles + 1):
                 @pl.when(count == w)
                 def _(w=w):
@@ -117,6 +138,8 @@
             def _():
                 per_width(q, first_down)
 
+        for c in small:
+            c.wait()
         for i in range(ne // LANES):
             line = active[0:1, i * LANES:(i + 1) * LANES].astype(jnp.float32)
             act_col[i * LANES:(i + 1) * LANES, :] = jnp.broadcast_to(line, (LANES, LANES)).T
@@ -217,10 +240,10 @@
             return remote(send_buf.at[tile_rows(q), c], land_l.at[tile_rows(q), c],
                           rsl_s.at[q], rsl_r.at[q], down)
 
-        def each_tile(block, make, act):
+        def each_tile(block, make, act, kind=FULL):
             for t in range(per):
                 q = block * per + t
-                per_width(q, lambda c, q=q: act(make(q, c)))
+                per_width(q, lambda c, q=q: act(make(q, c)), kind)
 
         def partial_step(k, ends):
             lo, hi = ends
@@ -240,11 +263,11 @@
 
             @pl.when(sends_up)
             def _():
-                each_tile(d, scatter_up, lambda c: c.start())
+                each_tile(d, scatter_up, lambda c: c.start(), UP)
 
             @pl.when(sends_down)
             def _():
-                each_tile(d, scatter_down, lambda c: c.start())
+                each_tile(d, scatter_down, lambda c: c.start(), DOWN)
 
             step_hi = use_hi.astype(jnp.int32)
             return lo + 1 - step_hi, hi - step_hi
@@ -265,7 +288,7 @@
                             gacc[tile_rows(q), c] + land_r[tile_rows(q), c].astype(jnp.float32)
                         ).astype(jnp.bfloat16)
                         scatter_up(q, c).start()
-                    per_width(q, add)
+                    per_width(q, add, UP)
 
             @pl.when(has_up & (slot >= n - 1 - z))
             def _():
@@ -279,20 +302,39 @@
                             gacc[tile_rows(q), c] + land_l[tile_rows(q), c].astype(jnp.float32)
                         ).astype(jnp.bfloat16)
                         scatter_down(q, c).start()
-                    per_width(q, add)
+                    per_width(q, add, DOWN)
 
         @pl.when(has_down)
         def _():
-            each_tile(z, scatter_up, lambda c: c.wait_recv())
+            each_tile(z, scatter_up, lambda c: c.wait_recv(), UP)
 
         @pl.when(has_up)
         def _():
-            each_tile(z, scatter_down, lambda c: c.wait_recv())
+            each_tile(z, scatter_down, lambda c: c.wait_recv(), DOWN)
 
         mine = pl.ds(row_of(z), rows)
+        def add_landed(land, there, q, mirrored):
+            inside, diag = square(q)
+            offset = lax.rem(q * tile, LANES)
+            for j in range(col_tiles):
+                c = slice(j * LANES, (j + 1) * LANES)
+                flip = inside & mirrored(j, diag)
+
+                @pl.when(there & jnp.logical_not(flip))
+                def _():
+                    gacc[tile_rows(q), c] += land[tile_rows(q), c].astype(jnp.float32)
+
+                @pl.when(there & flip)
+                def _():
+                    twin = pl.ds(pl.multiple_of(col0 + j * LANES, LANES), LANES)
+                    own = pl.ds(pl.multiple_of(diag * LANES, LANES), LANES)
+                    flipped[...] = land[twin, own].astype(jnp.float32).T
+                    gacc[tile_rows(q), c] += flipped[pl.ds(pl.multiple_of(offset, tile), tile), :]
+
+        for t in range(per):
+            add_landed(land_r, has_down, z * per + t, lambda j, diag: j > diag)
+            add_landed(land_l, has_up, z * per + t, lambda j, diag: j < diag)
         gradient = gacc[mine, :]
-        gradient = gradient + jnp.where(has_down, land_r[mine, :].astype(jnp.float32), 0.0)
-        gradient = gradient + jnp.where(has_up, land_l[mine, :].astype(jnp.float32), 0.0)
         data = allm[mine, :].astype(jnp.float32)
         out[...] = jnp.where(pair_mask(z), data - gain[0] * gradient, 0.0)
 
@@ -311,15 +353,21 @@
 
             @pl.when(has_up & (b > z))
             def _():
-                each_tile(b, scatter_up, lambda c: c.wait_send())
+                each_tile(b, scatter_up, lambda c: c.wait_send(), UP)
 
             @pl.when(has_down & (b < z))
             def _():
-                each_tile(b, scatter_down, lambda c: c.wait_send())
+                each_tile(b, scatter_down, lambda c: c.wait_send(), DOWN)
 
     tiles = n * per
     dma = pltpu.SemaphoreType.DMA
     scratch = [
+        pltpu.VMEM((1, ne), jnp.int32),
+        pltpu.SMEM((1,), jnp.int32),
+        pltpu.SMEM((1,), jnp.float32),
+        pltpu.SMEM((n_blocks,), jnp.int32),
+        pltpu.SMEM((regions,), jnp.float32),
+        dma((5,)),
         pltpu.VMEM((ne, cols), jnp.bfloat16),
         pltpu.VMEM((ne, vox_local), jnp.bfloat16),
         pltpu.VMEM((ne, LANES), jnp.float32),
@@ -329,6 +377,7 @@
         pltpu.VMEM((peers, 1, vox_local), jnp.float32),
         pltpu.VMEM((cols, vox_local), jnp.bfloat16),
         pltpu.VMEM((ne, cols), jnp.float32),
+        pltpu.VMEM((LANES, LANES), jnp.float32),
         pltpu.VMEM((ne, cols), jnp.bfloat16),
         pltpu.VMEM((ne, cols), jnp.bfloat16),
         pltpu.VMEM((ne, cols), jnp.bfloat16),
@@ -348,19 +397,18 @@
         _, ne, vox_local = green.shape
         kernel, scratch = make_kernel(
             sizes["vox"], sizes["freq"], sizes["sub"], rows, cols, ne, vox_local,
-            block_region.shape[0],
+            block_region.shape[0], strength.shape[0],
         )
         vmem = pl.BlockSpec(memory_space=pltpu.VMEM)
-        smem = pl.BlockSpec(memory_space=pltpu.SMEM)
-        any_space = pl.BlockSpec(memory_space=pl.ANY)
+        hbm = pl.BlockSpec(memory_space=pltpu.HBM)
         updated = pl.pallas_call(
             kernel,
             out_shape=jax.ShapeDtypeStruct((rows, cols), jnp.float32),
-            in_specs=[any_space, any_space, vmem, smem, smem, smem, smem],
+            in_specs=[hbm] * 7,
             out_specs=vmem,
             scratch_shapes=scratch,
             compiler_params=pltpu.CompilerParams(
-                collective_id=0, has_side_effects=True, vmem_limit_bytes=48 * 1024 * 1024
+                collective_id=0, has_side_effects=True, vmem_limit_bytes=60 * 1024 * 1024
             ),
             name="imaging_step",
         )(residual[0], green[0], active, aperture, step_gain, block_region, strength)

time: 51.8 us -> 46.9 us (0.905)
  local copies, waits for them, and re-layouts: 5.92 us -> 1.87 us
  Pallas kernels: 44.3 us -> 43.6 us
    unnamed x11 -> x1, local copies, waits for them, and re-layouts: 5.92 us -> 1.87 us
    pallas_call x1, Pallas kernels: 44.3 us -> 43.6 us  [body(): pl.pallas_call(kernel, out_shape=jax.ShapeDtypeStruct((rows, cols), jnp.f...]
where the time goes in v2:
time: 46.9 us; the launch traced here: 46.7 us
  Pallas kernels  43.6 us (93%)
  local copies, waits for them, and re-layouts  1.87 us (4%)
  between operations  1.3 us (3%)
    pallas_call x1, Pallas kernels, body(): pl.pallas_call(kernel, out_shape=jax.ShapeDtypeStruct((rows, cols), jnp.f...  43.6 us
    unnamed x1, local copies, waits for them, and re-layouts  1.87 us

profile of v2, /device:TPU:0, one launch (start us, length us, event | category | flops | bytes accessed | tf_op | source)
XLA Modules:
  0.0 46.7 jit_solution(1315065697064129500)
XLA Ops:
  1.3 43.6 %imaging_step.1 = f32[256,512]{1,0:T(8,128)} custom-call(bf16[256,512]{1,0:T(8,128)(2,1)} %bitcast.5, bf16[1024,2048]{1,0:T(8,128)(2,1)} %bitcast.3, s32[1,1024]{1,0:T(1,128)} %active_in.1, s32[1]{0:T(128)S(6)} %copy.9.aperture_in, f32[1]{0:T(128)S(6)} %copy.10.gain_in, s32[16]{0:T(128)} %region_in.1, f32[16]{0:T(128)} %strength_in.1), custom_call_target="tpu_custom_call" | custom-call | tf_op jit(solution)/shard_map/imaging_step/pallas_call | solution.py:404
  44.9 1.9 %copy.11 = f32[1,256,512]{2,1,0:T(8,128)} copy(f32[1,256,512]{2,1,0:T(8,128)} %bitcast.4) | data formatting | bytes 1048576

commit v3 on v2

--- a/solution.py
+++ b/solution.py
@@ -76,24 +76,23 @@
         def square(q):
             local = q * tile - s * cols
             inside = (local >= 0) & (local < cols)
-            return inside, jnp.clip(local, 0, cols - 1) // LANES
+            return inside, lax.div(jnp.clip(local, 0, cols - 1), LANES)
 
         def band(q, kind):
-            r0 = q * tile
-            inside, diag = square(q)
-            first = jnp.int32(0)
-            count = jnp.int32(0)
-            for j in range(col_tiles):
-                c0 = s * cols + j * LANES
-                below = c0 + LANES - 1 + APERTURE_MAX < r0
-                above = c0 > r0 + tile - 1 + APERTURE_MAX
-                if kind == UP:
-                    above = above | (inside & (j > diag))
-                if kind == DOWN:
-                    below = below | (inside & (j < diag))
-                first = first + below.astype(jnp.int32)
-                count = count + 1 - below.astype(jnp.int32) - above.astype(jnp.int32)
-            return first, count
+            reach = q * tile - s * cols + ne
+            shift = ne // LANES + APERTURE_MAX // LANES + 1
+            lift = LANES * (shift - ne // LANES)
+            first = lax.div(reach + lift - APERTURE_MAX, LANES) - shift
+            last = lax.div(reach + lift + tile - 1 + APERTURE_MAX, LANES) - shift + 1
+            first = jnp.clip(first, 0, col_tiles)
+            last = jnp.clip(last, 0, col_tiles)
+            if kind != FULL:
+                inside, diag = square(q)
+            if kind == UP:
+                last = jnp.where(inside, jnp.minimum(last, diag + 1), last)
+            if kind == DOWN:
+                first = jnp.where(inside, jnp.maximum(first, diag), first)
+            return first, last - first
 
         def per_width(q, fn, kind=FULL):
             first, count = band(q, kind)
@@ -110,6 +109,11 @@
                 src_ref=src, dst_ref=dst, send_sem=send, recv_sem=recv,
                 device_id=target, device_id_type=MESH,
             )
+
+        def each_tile(block, make, act, kind=FULL):
+            for t in range(per):
+                q = block * per + t
+                per_width(q, lambda c, q=q: act(make(q, c)), kind)
 
         def gather_up(q, c):
             a = allm.at[tile_rows(q), c]
@@ -217,6 +221,17 @@
         strength_map = jnp.concatenate(
             [jnp.full((1, BLOCK), strength[region[b]], jnp.float32) for b in range(n_blocks)], axis=1
         )
+
+        @pl.loop(0, n)
+        def _(b):
+            @pl.when(has_up & (b <= z))
+            def _():
+                each_tile(b, gather_up, lambda c: c.wait_send())
+
+            @pl.when(has_down & (b >= z))
+            def _():
+                each_tile(b, gather_down, lambda c: c.wait_send())
+
         for e in exchanges:
             e.wait_recv()
         total = ar_send[...]
@@ -239,11 +254,6 @@
         def scatter_down(q, c):
             return remote(send_buf.at[tile_rows(q), c], land_l.at[tile_rows(q), c],
                           rsl_s.at[q], rsl_r.at[q], down)
-
-        def each_tile(block, make, act, kind=FULL):
-            for t in range(per):
-                q = block * per + t
-                per_width(q, lambda c, q=q: act(make(q, c)), kind)
 
         def partial_step(k, ends):
             lo, hi = ends
@@ -343,14 +353,6 @@
 
         @pl.loop(0, n)
         def _(b):
-            @pl.when(has_up & (b <= z))
-            def _():
-                each_tile(b, gather_up, lambda c: c.wait_send())
-
-            @pl.when(has_down & (b >= z))
-            def _():
-                each_tile(b, gather_down, lambda c: c.wait_send())
-
             @pl.when(has_up & (b > z))
             def _():
                 each_tile(b, scatter_up, lambda c: c.wait_send(), UP)

time: 46.9 us -> 46.7 us (level)
  no operation moved by 1% of the time
where the time goes in v3:
time: 46.7 us; the launch traced here: 46.5 us
  Pallas kernels  43.3 us (93%)
  local copies, waits for them, and re-layouts  1.87 us (4%)
  between operations  1.3 us (3%)
    pallas_call x1, Pallas kernels, body(): pl.pallas_call(kernel, out_shape=jax.ShapeDtypeStruct((rows, cols), jnp.f...  43.3 us
    unnamed x1, local copies, waits for them, and re-layouts  1.87 us

profile of v3, /device:TPU:0, one launch (start us, length us, event | category | flops | bytes accessed | tf_op | source)
XLA Modules:
  0.0 46.5 jit_solution(18380856327958170035)
XLA Ops:
  1.3 43.3 %imaging_step.1 = f32[256,512]{1,0:T(8,128)} custom-call(bf16[256,512]{1,0:T(8,128)(2,1)} %bitcast.5, bf16[1024,2048]{1,0:T(8,128)(2,1)} %bitcast.3, s32[1,1024]{1,0:T(1,128)} %active_in.1, s32[1]{0:T(128)S(6)} %copy.9.aperture_in, f32[1]{0:T(128)S(6)} %copy.10.gain_in, s32[16]{0:T(128)} %region_in.1, f32[16]{0:T(128)} %strength_in.1), custom_call_target="tpu_custom_call" | custom-call | tf_op jit(solution)/shard_map/imaging_step/pallas_call | solution.py:406
  44.6 1.9 %copy.11 = f32[1,256,512]{2,1,0:T(8,128)} copy(f32[1,256,512]{2,1,0:T(8,128)} %bitcast.4) | data formatting | bytes 1048576
